TPU v7x, 32 devices: a whole 2x2x4 slice. The times are simulated.
32 devices in a mesh: dp: 4 (over z), graph: 8 (over y, x, core).
Axes of the slice: x: 2, y: 2, z: 4, core: 2. Of those that a mesh axis runs over, the one named last changes fastest.
Arguments:
- features: float32 [4, 128, 3200], P('dp', 'graph'), may hold values from -6 to 6
- cotangent: float32 [4, 128, 1600], P('dp', 'graph'), may hold values from -6 to 6
- rotation: bfloat16 [4, 114, 1536], P('dp', None, 'graph'), may hold values from -2.6875 to 2.6875
- send_left: int32 [4, 64], P('dp', 'graph'), may hold values from 0 to 16, as said below
- send_right: int32 [4, 64], P('dp', 'graph'), may hold values from 0 to 16, as said below
- edge_src: int32 [4, 1536], P('dp', 'graph'), may hold values from 0 to 31, as said below
- edge_tgt: int32 [4, 1536], P('dp', 'graph'), may hold values from 0 to 15, as said below
- w_zero: bfloat16 [640, 832], P('graph'), may hold values from -0.25 to 0.25
- w_one_re: bfloat16 [512, 256], P('graph'), may hold values from -0.1875 to 0.1875
- w_one_im: bfloat16 [512, 256], P('graph'), may hold values from -0.1875 to 0.1875
- w_two_re: bfloat16 [384, 192], P('graph'), may hold values from -0.21875 to 0.21875
- w_two_im: bfloat16 [384, 192], P('graph'), may hold values from -0.21875 to 0.21875
- w_target: bfloat16 [128, 512], P('graph'), may hold values from -0.5 to 0.5
- alpha_vec: bfloat16 [64, 8], P('graph'), may hold values from -0.75 to 0.75
Outputs:
- attended: bfloat16 [4, 128, 1600], P('dp', 'graph')
- grad_features: float32 [4, 128, 3200], P('dp', 'graph')
- grad_zero: float32 [640, 832], P('graph')
- grad_one_re: float32 [512, 256], P('graph')
- grad_one_im: float32 [512, 256], P('graph')
- grad_two_re: float32 [384, 192], P('graph')
- grad_two_im: float32 [384, 192], P('graph')
- grad_target: float32 [128, 512], P('graph')
- grad_alpha: float32 [64, 8], P('graph')
Inputs may be any that keep to these rules, and one draw needn't show every extreme that they name: `send_left`: filled slots come first and name distinct atoms; the value 16 marks an empty slot; each list holds 4 or more atoms, and in every cell some slab fills all 8 slots. `send_right`: like send_left. `edge_src`: values below 16 are the slab's own atoms; 16 + k is slot k of slab g-1's send_right, 24 + k slot k of slab g+1's send_left; never an empty slot. `edge_tgt`: every atom of a slab is the target of one edge or more.
All inputs are finite; a program needn't handle non-finite values.
Results may differ from a plain program's by a relative error of at most 0.0085.
Values may be sent and summed in bfloat16 or wider, within the bound.
A program may use at most 128 MiB of HBM per device.

v0:
```python
from functools import partial
import jax
import jax.numpy as jnp
from jax import lax
from jax.sharding import PartitionSpec as P


def padded_2(block, sides, width):
    for axis, dim in sides:
        count = lax.axis_size(axis)
        forward = [(i, i + 1) for i in range(count - 1)]
        forward.append((count - 1, 0))
        backward = [(target, source) for source, target in forward]
        low = lax.ppermute(
            lax.slice_in_dim(block, block.shape[dim] - width, None, axis=dim), axis, forward
        )
        high = lax.ppermute(lax.slice_in_dim(block, 0, width, axis=dim), axis, backward)
        block = jnp.concatenate([low, block, high], axis=dim)
    return block


def turn_blocks(rotation, edge_count):
    blocks = []
    offset = 0
    for degree in range(1, 5):
        kept_order = min(degree, 2)
        row_count = 2 * kept_order + 1
        column_count = 2 * degree + 1
        piece_block = rotation[offset : offset + row_count * column_count].astype(jnp.float32)
        blocks.append(piece_block.reshape(row_count, column_count, edge_count))
        offset = offset + row_count * column_count
    return blocks


def apply_block(block, source_part):
    rows_out = []
    for row in range(block.shape[0]):
        total = block[row, 0][:, None] * source_part[:, 0, :]
        for column in range(1, block.shape[1]):
            total = total + block[row, column][:, None] * source_part[:, column, :]
        rows_out.append(total)
    return jnp.stack(rows_out, axis=1)


def apply_back(block, stacked):
    columns_out = []
    for column in range(block.shape[1]):
        total = block[0, column][:, None] * stacked[:, 0, :]
        for row in range(1, block.shape[0]):
            total = total + block[row, column][:, None] * stacked[:, row, :]
        columns_out.append(total)
    return jnp.stack(columns_out, axis=1)


def pick_order(turned, azimuth, degrees, edge_count):
    chosen = jnp.stack(
        [turned[degree][:, min(degree, 2) + azimuth, :] for degree in degrees], axis=1
    )
    return chosen.reshape(edge_count, -1).astype(jnp.bfloat16)


def attend(
    extended,
    w_zero,
    w_one_re,
    w_one_im,
    w_two_re,
    w_two_im,
    w_target,
    alpha_vec,
    rotation,
    edge_src,
    edge_tgt,
    atom_count,
):
    edge_count = edge_src.shape[0]
    channels = w_target.shape[0]
    hidden = w_one_re.shape[1] // 4
    head_count = alpha_vec.shape[1]
    alpha_width = alpha_vec.shape[0]
    blocks = turn_blocks(rotation, edge_count)
    coeffs = extended.reshape(extended.shape[0], 25, channels)
    turned = [jnp.take(coeffs[:, 0:1, :], edge_src, axis=0)]
    for degree in range(1, 5):
        source_part = jnp.take(
            coeffs[:, degree * degree : (degree + 1) * (degree + 1), :], edge_src, axis=0
        )
        turned.append(apply_block(blocks[degree - 1], source_part))
    zero_in = pick_order(turned, 0, range(5), edge_count)
    one_pos = pick_order(turned, 1, range(1, 5), edge_count)
    one_neg = pick_order(turned, -1, range(1, 5), edge_count)
    two_pos = pick_order(turned, 2, range(2, 5), edge_count)
    two_neg = pick_order(turned, -2, range(2, 5), edge_count)
    mixed = jnp.dot(zero_in, w_zero, preferred_element_type=jnp.float32)
    hidden_zero = mixed[:, : 5 * hidden].reshape(edge_count, 5, hidden)
    target_in = extended[:atom_count, :channels].astype(jnp.bfloat16)
    per_atom = jnp.dot(target_in, w_target, preferred_element_type=jnp.float32)
    alpha_pre = mixed[:, 5 * hidden :] + jnp.take(per_atom, edge_tgt, axis=0)
    one_up = jnp.dot(one_pos, w_one_re, preferred_element_type=jnp.float32) - jnp.dot(
        one_neg, w_one_im, preferred_element_type=jnp.float32
    )
    one_down = jnp.dot(one_neg, w_one_re, preferred_element_type=jnp.float32) + jnp.dot(
        one_pos, w_one_im, preferred_element_type=jnp.float32
    )
    two_up = jnp.dot(two_pos, w_two_re, preferred_element_type=jnp.float32) - jnp.dot(
        two_neg, w_two_im, preferred_element_type=jnp.float32
    )
    two_down = jnp.dot(two_neg, w_two_re, preferred_element_type=jnp.float32) + jnp.dot(
        two_pos, w_two_im, preferred_element_type=jnp.float32
    )
    scalar = hidden_zero[:, 0, :]
    gating = jax.nn.sigmoid(scalar)[:, None, :]
    value_zero = jnp.concatenate(
        [jax.nn.silu(scalar)[:, None, :], hidden_zero[:, 1:, :] * gating], axis=1
    )
    one_up = one_up.reshape(edge_count, 4, hidden) * gating
    one_down = one_down.reshape(edge_count, 4, hidden) * gating
    two_up = two_up.reshape(edge_count, 3, hidden) * gating
    two_down = two_down.reshape(edge_count, 3, hidden) * gating
    scores = alpha_pre.reshape(edge_count, head_count, alpha_width)
    centre = scores - jnp.mean(scores, axis=-1, keepdims=True)
    normed = centre * lax.rsqrt(jnp.mean(centre * centre, axis=-1, keepdims=True) + 1e-05)
    activated = normed * (0.2 + 0.8 * jax.nn.sigmoid(normed))
    logits = jnp.einsum(
        "ehc,ch->eh", activated, alpha_vec.astype(jnp.float32), precision=lax.Precision.HIGHEST
    )
    raised = jnp.exp(logits)
    member = (edge_tgt[:, None] == jnp.arange(atom_count, dtype=jnp.int32)[None, :]).astype(
        jnp.float32
    )
    totals = jnp.dot(member.T, raised, precision=lax.Precision.HIGHEST)
    weights = raised / jnp.take(totals, edge_tgt, axis=0)
    spread = jnp.repeat(weights, hidden // head_count, axis=1)[:, None, :]
    value_zero = value_zero * spread
    one_up = one_up * spread
    one_down = one_down * spread
    two_up = two_up * spread
    two_down = two_down * spread
    pieces = [value_zero[:, 0:1, :]]
    for degree in range(1, 5):
        kept_order = min(degree, 2)
        row_list = []
        for azimuth in range(-kept_order, kept_order + 1):
            if azimuth == 0:
                row_list.append(value_zero[:, degree])
            elif azimuth == 1:
                row_list.append(one_up[:, degree - 1])
            elif azimuth == -1:
                row_list.append(one_down[:, degree - 1])
            elif azimuth == 2:
                row_list.append(two_up[:, degree - 2])
            else:
                row_list.append(two_down[:, degree - 2])
        stacked = jnp.stack(row_list, axis=1)
        pieces.append(apply_back(blocks[degree - 1], stacked))
    message = jnp.concatenate(pieces, axis=1).reshape(edge_count, -1).astype(jnp.bfloat16)
    return jnp.dot(member.T.astype(jnp.bfloat16), message, preferred_element_type=jnp.float32)


def body(
    features,
    cotangent,
    rotation,
    send_left,
    send_right,
    edge_src,
    edge_tgt,
    w_zero,
    w_one_re,
    w_one_im,
    w_two_re,
    w_two_im,
    w_target,
    alpha_vec,
):
    full_weights = (
        lax.all_gather(w_zero, "graph", axis=0, tiled=True),
        lax.all_gather(w_one_re, "graph", axis=0, tiled=True),
        lax.all_gather(w_one_im, "graph", axis=0, tiled=True),
        lax.all_gather(w_two_re, "graph", axis=0, tiled=True),
        lax.all_gather(w_two_im, "graph", axis=0, tiled=True),
        lax.all_gather(w_target, "graph", axis=0, tiled=True),
        lax.all_gather(alpha_vec, "graph", axis=0, tiled=True),
    )
    own_rows = features[0]
    atom_count = own_rows.shape[0]
    ghost_count = send_left.shape[1]
    row_width = own_rows.shape[1]
    padded = jnp.concatenate([own_rows, jnp.zeros((1, row_width), jnp.float32)], axis=0)
    outgoing = jnp.concatenate(
        [jnp.take(padded, send_left[0], axis=0), jnp.take(padded, send_right[0], axis=0)], axis=0
    )
    widened = padded_2(outgoing, (("graph", 0),), ghost_count)
    extended = jnp.concatenate(
        [own_rows, widened[:ghost_count], widened[3 * ghost_count :]], axis=0
    )
    local_fn = partial(
        attend,
        rotation=rotation[0],
        edge_src=edge_src[0],
        edge_tgt=edge_tgt[0],
        atom_count=atom_count,
    )
    summed, pullback = jax.vjp(
        local_fn,
        extended,
        full_weights[0],
        full_weights[1],
        full_weights[2],
        full_weights[3],
        full_weights[4],
        full_weights[5],
        full_weights[6],
    )
    pulled = pullback(cotangent[0])
    ext_grad = pulled[0]
    returned = padded_2(
        ext_grad[atom_count:].astype(jnp.bfloat16), (("graph", 0),), ghost_count
    ).astype(jnp.float32)
    collected = jnp.concatenate(
        [ext_grad[:atom_count], jnp.zeros((1, row_width), jnp.float32)], axis=0
    )
    collected = collected.at[send_left[0]].add(returned[:ghost_count])
    collected = collected.at[send_right[0]].add(returned[3 * ghost_count :])
    grad_features = collected[:atom_count][None]
    grad_terms = tuple((term.astype(jnp.float32) for term in pulled[1:]))
    shard_refs = (w_zero, w_one_re, w_one_im, w_two_re, w_two_im, w_target, alpha_vec)
    grand_totals = lax.psum(grad_terms, ("dp", "graph"))
    position = lax.axis_index("graph")
    shards = tuple(
        (
            lax.dynamic_slice_in_dim(
                summed_all, position * shard_ref.shape[0], shard_ref.shape[0], 0
            )
            for summed_all, shard_ref in zip(grand_totals, shard_refs)
        )
    )
    attended = summed.astype(jnp.bfloat16)[None]
    return (
        attended,
        grad_features,
        shards[0],
        shards[1],
        shards[2],
        shards[3],
        shards[4],
        shards[5],
        shards[6],
    )


def solution(mesh):
    in_specs = (
        P("dp", "graph", None),
        P("dp", "graph", None),
        P("dp", None, "graph"),
        P("dp", "graph"),
        P("dp", "graph"),
        P("dp", "graph"),
        P("dp", "graph"),
        P("graph", None),
        P("graph", None),
        P("graph", None),
        P("graph", None),
        P("graph", None),
        P("graph", None),
        P("graph", None),
    )
    out_specs = (
        P("dp", "graph", None),
        P("dp", "graph", None),
        P("graph", None),
        P("graph", None),
        P("graph", None),
        P("graph", None),
        P("graph", None),
        P("graph", None),
        P("graph", None),
    )
    return jax.shard_map(body, mesh=mesh, in_specs=in_specs, out_specs=out_specs, check_vma=False)
```

profile of v0, /device:TPU:0, one launch (start us, length us, event | category | flops | bytes accessed | tf_op | source)
XLA Modules:
  0.0 474.5 jit_solution(5100000157046764141)
XLA Ops:
  11.7 3.4 collective-permute-start.1
  25.2 9.0 %all_gather.23 = bf16[64,8]{1,0:T(8,128)(2,1)S(1)} all-gather(bf16[8,8]{1,0:T(8,128)(2,1)S(1)} %copy-done.539), channel_id=1, replica_groups=mesh['dp'=4,'graph'=8] {'graph'}, dimensions={0}, use_global_device_ids=true | all-gather | bytes 1152 | tf_op jit(solution)/shard_map/all_gather | solution.py:183
  35.0 8.3 %all_gather.22 = bf16[128,512]{1,0:T(8,128)(2,1)S(1)} all-gather(bf16[16,512]{1,0:T(8,128)(2,1)S(1)} %copy-done.528), channel_id=1, replica_groups=mesh['dp'=4,'graph'=8] {'graph'}, dimensions={0}, use_global_device_ids=true | all-gather | bytes 147456 | tf_op jit(solution)/shard_map/all_gather | solution.py:182
  43.4 10.1 %all_gather.26 = bf16[384,192]{1,0:T(8,128)(2,1)} all-gather(bf16[48,192]{1,0:T(8,128)(2,1)S(1)} %copy-done.524), channel_id=1, replica_groups=mesh['dp'=4,'graph'=8] {'graph'}, dimensions={0}, use_global_device_ids=true | all-gather | bytes 165888 | tf_op jit(solution)/shard_map/all_gather | solution.py:180
  53.5 8.4 %all_gather.27 = bf16[384,192]{1,0:T(8,128)(2,1)S(1)} all-gather(bf16[48,192]{1,0:T(8,128)(2,1)S(1)} %copy-done.525), channel_id=1, replica_groups=mesh['dp'=4,'graph'=8] {'graph'}, dimensions={0}, use_global_device_ids=true | all-gather | bytes 165888 | tf_op jit(solution)/shard_map/all_gather | solution.py:181
  61.8 10.2 %all_gather.24 = bf16[512,256]{1,0:T(8,128)(2,1)} all-gather(bf16[64,256]{1,0:T(8,128)(2,1)S(1)} %copy-done.190), channel_id=1, replica_groups=mesh['dp'=4,'graph'=8] {'graph'}, dimensions={0}, use_global_device_ids=true | all-gather | bytes 294912 | tf_op jit(solution)/shard_map/all_gather | solution.py:178
  72.0 9.5 %all_gather.25 = bf16[512,256]{1,0:T(8,128)(2,1)} all-gather(bf16[64,256]{1,0:T(8,128)(2,1)S(1)} %copy-done.191), channel_id=1, replica_groups=mesh['dp'=4,'graph'=8] {'graph'}, dimensions={0}, use_global_device_ids=true | all-gather | bytes 294912 | tf_op jit(solution)/shard_map/all_gather | solution.py:179
  86.0 1.8 gather_fusion.5
  92.9 1.3 pad_maximum_fusion.9
  102.8 2.0 gather_fusion.4
  105.1 1.7 copy_select_fusion
  109.8 1.4 constant_dynamic-update-slice_fusion.4
  113.0 1.6 multiply_add_fusion.14
  114.6 1.6 constant_dynamic-update-slice_fusion.2
  125.8 1.8 fusion.145
  138.6 1.1 multiply_reduce_fusion.2
  139.8 1.6 slice_multiply_fusion
  141.6 1.3 scatter_custom_fusion
  145.5 2.6 scatter_custom_fusion.1
  148.9 1.6 fusion.17
  152.7 2.3 fusion.126
  155.0 1.8 reshape.3774
  156.8 2.3 fusion.127
  159.1 1.1 fusion.88
  161.9 1.4 fusion.3
  163.2 1.3 copy.189
  165.4 1.6 copy.223
  167.0 2.0 fusion.11
  169.0 1.9 fusion.9
  171.0 1.1 reshape.3776
  172.1 1.1 reshape.3778
  175.3 1.0 pad_add_fusion.9
  176.4 1.2 slice_multiply_fusion.89
  177.8 1.3 slice_multiply_fusion.98
  179.2 1.2 slice_multiply_fusion.107
  180.4 1.9 slice_multiply_fusion.116
  182.5 1.2 slice_multiply_fusion.125
  185.7 1.9 slice_multiply_fusion.49
  187.7 1.2 slice_multiply_fusion.56
  189.0 1.2 slice_multiply_fusion.63
  190.3 1.2 slice_multiply_fusion.70
  193.4 1.7 slice_multiply_fusion.25
  195.1 1.9 slice_multiply_fusion.30
  197.1 1.2 slice_multiply_fusion.35
  198.4 1.9 fusion.2
  203.6 40.3 %psum.55 = f32[64,8]{1,0:T(8,128)} all-reduce(f32[64,8]{1,0:T(8,128)S(1)} %convert_bitcast_fusion), channel_id=1, replica_groups=mesh['dp'=4,'graph'=8] {'dp','graph'}, use_global_device_ids=true, to_apply=%region_30.32 | all-reduce | flops 512 | bytes 4096 | tf_op jit(solution)/shard_map/psum | solution.py:228
  245.1 2.1 scatter_custom_fusion.6
  247.3 2.0 fusion.7
  249.3 1.1 fusion.5
  267.3 2.0 pad_add_fusion
  271.0 1.9 pad_add_fusion.4
  274.1 13.1 %scatter_fusion.3 = f32[32,3,128]{2,1,0:T(4,128)S(1)} fusion(f32[32,3,128]{2,1,0:T(4,128)S(1)} %broadcast_in_dim.136, s32[192]{0:T(256)S(1)} %bitcast.473, f32[192,3,128]{2,1,0:T(4,128)} %copy.207), kind=kCustom, calls=%fused_computation.14 | custom fusion | flops 73728 | bytes 885504 | tf_op jit(solution)/shard_map/transpose(jvp(jit(_take)))/scatter-add | solution.py:85
  287.3 7.6 %scatter_fusion = f32[32,9,128]{2,1,0:T(8,128)S(1)} fusion(f32[32,9,128]{2,1,0:T(8,128)S(1)} %broadcast_in_dim.133, s32[192]{0:T(256)S(1)} %bitcast.474, f32[192,9,128]{2,1,0:T(8,128)S(1)} %copy.191), kind=kCustom, calls=%fused_computation.11 | custom fusion | flops 221184 | bytes 2654976 | tf_op jit(solution)/shard_map/transpose(jvp(jit(_take)))/scatter-add | solution.py:85
  294.9 7.2 %scatter_fusion.1 = f32[32,7,128]{2,1,0:T(8,128)S(1)} fusion(f32[32,7,128]{2,1,0:T(8,128)S(1)} %broadcast_in_dim.134, s32[192]{0:T(256)S(1)} %bitcast.475, f32[192,7,128]{2,1,0:T(8,128)S(1)} %copy.197), kind=kCustom, calls=%fused_computation.12 | custom fusion | flops 172032 | bytes 2065152 | tf_op jit(solution)/shard_map/transpose(jvp(jit(_take)))/scatter-add | solution.py:85
  302.2 7.2 %scatter_fusion.2 = f32[32,5,128]{2,1,0:T(8,128)S(1)} fusion(f32[32,5,128]{2,1,0:T(8,128)S(1)} %broadcast_in_dim.135, s32[192]{0:T(256)S(1)} %bitcast.476, f32[192,5,128]{2,1,0:T(8,128)S(1)} %copy.203), kind=kCustom, calls=%fused_computation.13 | custom fusion | flops 122880 | bytes 1475328 | tf_op jit(solution)/shard_map/transpose(jvp(jit(_take)))/scatter-add | solution.py:85
  309.9 2.6 collective-permute-start.3
  313.6 1.3 constant_dynamic-slice_fusion
  317.6 140.6 %all-reduce.276.cloned.1.call-done = (f32[640,832]{1,0:T(8,128)}, f32[512,256]{1,0:T(8,128)}, f32[512,256]{1,0:T(8,128)}, f32[384,192]{1,0:T(8,128)}, f32[384,192]{1,0:T(8,128)}, /*index=5*/f32[128,512]{0,1:T(8,128)}) async-done(((f32[640,832]{1,0:T(8,128)}, f32[512,256]{1,0:T(8,128)}, f32[512,256]{1,0:T(8,128)}, f32[384,192]{1,0:T(8,128)}, f32[384,192]{1,0:T(8,128)}, /*index=5*/f32[128,512]{0,1:T(8,128)}), ...) | async-done | bytes 4030480 | tf_op jit(solution)/shard_map/psum | solution.py:228
  458.2 1.4 constant_dynamic-slice_fusion.3
  459.6 1.4 constant_dynamic-slice_fusion.2
  461.0 1.5 constant_dynamic-slice_fusion.5
  462.5 1.5 constant_dynamic-slice_fusion.4
  464.0 1.1 constant_dynamic-slice_fusion.1
  465.8 1.7 constant_dynamic-slice_fusion.6
  (1309 shorter events, 96.3 us)
Async XLA Ops:
  7.2 74.5 %copy-start = (f32[1,16,1600]{2,1,0:T(8,128)S(1)}, f32[1,16,1600]{2,1,0:T(8,128)}, u32[]{:S(2)}) copy-start(f32[1,16,1600]{2,1,0:T(8,128)} %param.17) | copy-start | bytes 307204
  7.2 9.7 %copy-start.541 = (s32[1,8]{1,0:T(1,128)S(1)}, s32[1,8]{1,0:T(1,128)}, u32[]{:S(2)}) copy-start(s32[1,8]{1,0:T(1,128)} %param.20) | copy-start | bytes 100
  7.2 9.2 %copy-start.540 = (s32[1,8]{1,0:T(1,128)S(1)}, s32[1,8]{1,0:T(1,128)}, u32[]{:S(2)}) copy-start(s32[1,8]{1,0:T(1,128)} %param.19) | copy-start | bytes 100
  7.2 10.3 %copy-start.30 = (bf16[1,114,192]{1,2,0:T(8,128)(2,1)S(1)}, bf16[1,114,192]{1,2,0:T(8,128)(2,1)}, u32[]{:S(2)}) copy-start(bf16[1,114,192]{1,2,0:T(8,128)(2,1)} %param.18) | copy-start | bytes 131332
  7.2 118.5 %all-gather.2.cloned.1.call-start = ((), (), s32[]{:S(2)}) async-start(), calls=%async_computation | async-start | bytes 1290240 | tf_op jit(solution)/shard_map/all_gather | solution.py:177
  8.0 450.2 %all-reduce.276.cloned.1.call-start = ((), (), s32[]{:S(2)}) async-start(), calls=%async_computation.1 | async-start | bytes 8781824 | tf_op jit(solution)/shard_map/psum | solution.py:228
  10.3 12.3 %copy-start.25 = (f32[1,16,3200]{2,1,0:T(8,128)S(1)}, f32[1,16,3200]{2,1,0:T(8,128)}, u32[]{:S(2)}) copy-start(f32[1,16,3200]{2,1,0:T(8,128)} %param.16) | copy-start | bytes 614404
  10.3 12.4 %copy-start.542 = (s32[1,192]{1,0:T(1,128)S(1)}, s32[1,192]{1,0:T(1,128)}, u32[]{:S(2)}) copy-start(s32[1,192]{1,0:T(1,128)} %param.21) | copy-start | bytes 2308
  10.3 12.9 %copy-start.531 = (s32[1,192]{1,0:T(1,128)S(1)}, s32[1,192]{1,0:T(1,128)}, u32[]{:S(2)}) copy-start(s32[1,192]{1,0:T(1,128)} %param.22) | copy-start | bytes 2308
  11.0 14.3 %copy-start.539 = (bf16[8,8]{1,0:T(8,128)(2,1)S(1)}, bf16[8,8]{1,0:T(8,128)(2,1)}, u32[]{:S(2)}) copy-start(bf16[8,8]{1,0:T(8,128)(2,1)} %param.29) | copy-start | bytes 388
  11.0 24.0 %copy-start.528 = (bf16[16,512]{1,0:T(8,128)(2,1)S(1)}, bf16[16,512]{1,0:T(8,128)(2,1)}, u32[]{:S(2)}) copy-start(bf16[16,512]{1,0:T(8,128)(2,1)} %param.28) | copy-start | bytes 49156
  11.0 32.4 %copy-start.524 = (bf16[48,192]{1,0:T(8,128)(2,1)S(1)}, bf16[48,192]{1,0:T(8,128)(2,1)}, u32[]{:S(2)}) copy-start(bf16[48,192]{1,0:T(8,128)(2,1)} %param.26) | copy-start | bytes 55300
  11.7 80.4 %collective-permute-start.1 = (f32[8,3200]{1,0:T(8,128)}, f32[8,3200]{1,0:T(8,128)}, u32[]{:S(2)}, u32[]{:S(2)}) collective-permute-start(f32[8,3200]{1,0:T(8,128)} %broadcast_select_fusion), channel_id=1, source_target_pairs={{1,0},{2,1},{3,2},{4,3},{5,4},{6,5},{7,6},{0,7},{9,8},{10,9},{11,1... | collective-permute-start | bytes 307208 | tf_op jit(solution)/shard_map/ppermute | solution.py:17
  15.1 38.4 %copy-start.525 = (bf16[48,192]{1,0:T(8,128)(2,1)S(1)}, bf16[48,192]{1,0:T(8,128)(2,1)}, u32[]{:S(2)}) copy-start(bf16[48,192]{1,0:T(8,128)(2,1)} %param.27) | copy-start | bytes 55300
  15.1 46.8 %copy-start.190 = (bf16[64,256]{1,0:T(8,128)(2,1)S(1)}, bf16[64,256]{1,0:T(8,128)(2,1)}, u32[]{:S(2)}) copy-start(bf16[64,256]{1,0:T(8,128)(2,1)} %param.24) | copy-start | bytes 98308
  15.7 56.3 %copy-start.191 = (bf16[64,256]{1,0:T(8,128)(2,1)S(1)}, bf16[64,256]{1,0:T(8,128)(2,1)}, u32[]{:S(2)}) copy-start(bf16[64,256]{1,0:T(8,128)(2,1)} %param.25) | copy-start | bytes 98308
  16.4 75.7 %collective-permute-start = (f32[8,3200]{1,0:T(8,128)}, f32[8,3200]{1,0:T(8,128)}, u32[]{:S(2)}, u32[]{:S(2)}) collective-permute-start(f32[8,3200]{1,0:T(8,128)} %broadcast_select_fusion.1), channel_id=1, source_target_pairs={{0,1},{1,2},{2,3},{3,4},{4,5},{5,6},{6,7},{7,0},{8,9},{9,10},{10,1... | collective-permute-start | bytes 307208 | tf_op jit(solution)/shard_map/ppermute | solution.py:14
  18.3 80.3 %copy-start.195 = (f32[1,1,192]{2,1,0:T(1,128)}, f32[1,1,192]{2,1,0:T(1,128)S(1)}, u32[]{:S(2)}) copy-start(f32[1,1,192]{2,1,0:T(1,128)S(1)} %get-tuple-element.450) | copy-start | bytes 2308
  18.3 80.3 %copy-start.201 = (f32[1,1,192]{2,1,0:T(1,128)}, f32[1,1,192]{2,1,0:T(1,128)S(1)}, u32[]{:S(2)}) copy-start(f32[1,1,192]{2,1,0:T(1,128)S(1)} %get-tuple-element.451) | copy-start | bytes 2308
  18.3 80.3 %copy-start.207 = (f32[1,1,192]{2,1,0:T(1,128)}, f32[1,1,192]{2,1,0:T(1,128)S(1)}, u32[]{:S(2)}) copy-start(f32[1,1,192]{2,1,0:T(1,128)S(1)} %get-tuple-element.452) | copy-start | bytes 2308
  18.3 97.8 %copy-start.192 = (f32[1,1,192]{2,1,0:T(1,128)}, f32[1,1,192]{2,1,0:T(1,128)S(1)}, u32[]{:S(2)}) copy-start(f32[1,1,192]{2,1,0:T(1,128)S(1)} %get-tuple-element.455) | copy-start | bytes 2308
  18.3 97.8 %copy-start.198 = (f32[1,1,192]{2,1,0:T(1,128)}, f32[1,1,192]{2,1,0:T(1,128)S(1)}, u32[]{:S(2)}) copy-start(f32[1,1,192]{2,1,0:T(1,128)S(1)} %get-tuple-element.456) | copy-start | bytes 2308
  18.4 97.8 %copy-start.204 = (f32[1,1,192]{2,1,0:T(1,128)}, f32[1,1,192]{2,1,0:T(1,128)S(1)}, u32[]{:S(2)}) copy-start(f32[1,1,192]{2,1,0:T(1,128)S(1)} %get-tuple-element.457) | copy-start | bytes 2308
  23.3 10.9 %copy-start.538 = (s32[192,1]{0,1:T(1,128)}, s32[192,1]{0,1:T(1,128)S(1)}, u32[]{:S(2)}) copy-start(s32[192,1]{0,1:T(1,128)S(1)} %get-tuple-element.471) | copy-start | bytes 2308
  23.3 68.8 %copy-start.188 = (s32[192,1]{0,1:T(1,128)}, s32[192,1]{0,1:T(1,128)S(1)}, u32[]{:S(2)}) copy-start(s32[192,1]{0,1:T(1,128)S(1)} %get-tuple-element.472) | copy-start | bytes 2308
  43.2 38.4 %copy-start.23 = (bf16[128,512]{1,0:T(8,128)(2,1)}, bf16[128,512]{1,0:T(8,128)(2,1)S(1)}, u32[]{:S(2)}) copy-start(bf16[128,512]{1,0:T(8,128)(2,1)S(1)} %all_gather.22) | copy-start | bytes 393220
  92.1 10.7 %copy-start.526 = (s32[1024]{0:T(1024)}, s32[1024]{0:T(1024)S(1)}, u32[]{:S(2)}) copy-start(s32[1024]{0:T(1024)S(1)} %pad_clamp_fusion.1) | copy-start | bytes 12292
  102.7 22.1 %copy-start.58 = (bf16[192,1,128]{2,0,1:T(8,128)(2,1)}, bf16[192,1,128]{2,0,1:T(8,128)(2,1)S(1)}, u32[]{:S(2)}) copy-start(bf16[192,1,128]{2,0,1:T(8,128)(2,1)S(1)} %multiply_add_fusion.6) | copy-start | bytes 147460
  127.8 12.0 %copy-start.4 = (f32[192,320]{0,1:T(8,128)}, f32[192,320]{0,1:T(8,128)S(1)}, u32[]{:S(2)}) copy-start(f32[192,320]{0,1:T(8,128)S(1)} %copy.171) | copy-start | bytes 737284
  128.5 15.6 %copy-start.161 = (f32[192,8]{0,1:T(8,128)}, f32[192,8]{0,1:T(8,128)S(1)}, u32[]{:S(2)}) copy-start(f32[192,8]{0,1:T(8,128)S(1)} %fusion.106) | copy-start | bytes 18436
  152.7 9.2 %copy-start.3 = (bf16[640,832]{1,0:T(8,128)(2,1)S(1)}, bf16[640,832]{1,0:T(8,128)(2,1)}, u32[]{:S(2)}) copy-start(bf16[640,832]{1,0:T(8,128)(2,1)} %all-gather.2.cloned.1.call-done) | copy-start | bytes 3194884
  202.7 41.2 %copy-start.163 = (bf16[192,4,64]{0,2,1:T(8,128)(2,1)S(1)}, bf16[192,4,64]{0,2,1:T(8,128)(2,1)}, u32[]{:S(2)}) copy-start(bf16[192,4,64]{0,2,1:T(8,128)(2,1)} %get-tuple-element.64) | copy-start | bytes 294916
  202.7 41.2 %copy-start.169 = (bf16[192,1,128]{2,0,1:T(8,128)(2,1)S(1)}, bf16[192,1,128]{2,0,1:T(8,128)(2,1)}, u32[]{:S(2)}) copy-start(bf16[192,1,128]{2,0,1:T(8,128)(2,1)} %multiply_add_fusion.11) | copy-start | bytes 147460
  202.7 41.2 %copy-start.174 = (bf16[192,1,128]{2,0,1:T(8,128)(2,1)S(1)}, bf16[192,1,128]{2,0,1:T(8,128)(2,1)}, u32[]{:S(2)}) copy-start(bf16[192,1,128]{2,0,1:T(8,128)(2,1)} %multiply_add_fusion.12) | copy-start | bytes 147460
  202.7 41.2 %copy-start.179 = (bf16[192,1,128]{2,0,1:T(8,128)(2,1)S(1)}, bf16[192,1,128]{2,0,1:T(8,128)(2,1)}, u32[]{:S(2)}) copy-start(bf16[192,1,128]{2,0,1:T(8,128)(2,1)} %multiply_add_fusion.13) | copy-start | bytes 147460
  202.7 41.2 %copy-start.184 = (bf16[192,1,128]{2,0,1:T(8,128)(2,1)S(1)}, bf16[192,1,128]{2,0,1:T(8,128)(2,1)}, u32[]{:S(2)}) copy-start(bf16[192,1,128]{2,0,1:T(8,128)(2,1)} %copy-done.183) | copy-start | bytes 147460
  202.7 42.2 %copy-start.50 = (f32[192,1,128]{0,2,1:T(8,128)S(1)}, f32[192,1,128]{0,2,1:T(8,128)}, u32[]{:S(2)}) copy-start(f32[192,1,128]{0,2,1:T(8,128)} %get-tuple-element.185) | copy-start | bytes 294916
  202.7 42.3 %copy-start.49 = (f32[192,1,128]{0,2,1:T(8,128)S(1)}, f32[192,1,128]{0,2,1:T(8,128)}, u32[]{:S(2)}) copy-start(f32[192,1,128]{0,2,1:T(8,128)} %get-tuple-element.188) | copy-start | bytes 294916
  202.7 44.4 %copy-start.172 = (bf16[192,1,128]{2,0,1:T(8,128)(2,1)S(1)}, bf16[192,1,128]{2,0,1:T(8,128)(2,1)}, u32[]{:S(2)}) copy-start(bf16[192,1,128]{2,0,1:T(8,128)(2,1)} %multiply_add_fusion.7) | copy-start | bytes 147460
  202.7 44.4 %copy-start.177 = (bf16[192,1,128]{2,0,1:T(8,128)(2,1)S(1)}, bf16[192,1,128]{2,0,1:T(8,128)(2,1)}, u32[]{:S(2)}) copy-start(bf16[192,1,128]{2,0,1:T(8,128)(2,1)} %multiply_add_fusion.8) | copy-start | bytes 147460
  202.7 44.4 %copy-start.182 = (bf16[192,1,128]{2,0,1:T(8,128)(2,1)S(1)}, bf16[192,1,128]{2,0,1:T(8,128)(2,1)}, u32[]{:S(2)}) copy-start(bf16[192,1,128]{2,0,1:T(8,128)(2,1)} %multiply_add_fusion.9) | copy-start | bytes 147460
  202.7 44.4 %copy-start.187 = (bf16[192,1,128]{2,0,1:T(8,128)(2,1)S(1)}, bf16[192,1,128]{2,0,1:T(8,128)(2,1)}, u32[]{:S(2)}) copy-start(bf16[192,1,128]{2,0,1:T(8,128)(2,1)} %copy-done.185) | copy-start | bytes 147460
  203.4 45.9 %copy-start.545 = (bf16[512,256]{1,0:T(8,128)(2,1)S(1)}, bf16[512,256]{1,0:T(8,128)(2,1)}, u32[]{:S(2)}) copy-start(bf16[512,256]{1,0:T(8,128)(2,1)} %convolution_convert_fusion.5) | copy-start | bytes 786436
  258.6 8.2 %copy-start.151 = (f32[192,1,128]{2,0,1:T(8,128)S(1)}, f32[192,1,128]{2,0,1:T(8,128)}, u32[]{:S(2)}) copy-start(f32[192,1,128]{2,0,1:T(8,128)} %get-tuple-element.191) | copy-start | bytes 294916
  258.6 8.2 %copy-start.152 = (f32[192,1,128]{2,0,1:T(8,128)S(1)}, f32[192,1,128]{2,0,1:T(8,128)}, u32[]{:S(2)}) copy-start(f32[192,1,128]{2,0,1:T(8,128)} %get-tuple-element.192) | copy-start | bytes 294916
  258.7 8.1 %copy-start.147 = (f32[192,1,128]{2,0,1:T(8,128)S(1)}, f32[192,1,128]{2,0,1:T(8,128)}, u32[]{:S(2)}) copy-start(f32[192,1,128]{2,0,1:T(8,128)} %get-tuple-element.205) | copy-start | bytes 294916
  258.8 8.1 %copy-start.148 = (f32[192,1,128]{2,0,1:T(8,128)S(1)}, f32[192,1,128]{2,0,1:T(8,128)}, u32[]{:S(2)}) copy-start(f32[192,1,128]{2,0,1:T(8,128)} %get-tuple-element.206) | copy-start | bytes 294916
  258.8 8.1 %copy-start.149 = (f32[192,1,128]{2,0,1:T(8,128)S(1)}, f32[192,1,128]{2,0,1:T(8,128)}, u32[]{:S(2)}) copy-start(f32[192,1,128]{2,0,1:T(8,128)} %get-tuple-element.189) | copy-start | bytes 294916
  258.8 8.1 %copy-start.150 = (f32[192,1,128]{2,0,1:T(8,128)S(1)}, f32[192,1,128]{2,0,1:T(8,128)}, u32[]{:S(2)}) copy-start(f32[192,1,128]{2,0,1:T(8,128)} %get-tuple-element.190) | copy-start | bytes 294916
  258.8 8.1 %copy-start.113 = (f32[192,1,128]{2,0,1:T(8,128)S(1)}, f32[192,1,128]{2,0,1:T(8,128)}, u32[]{:S(2)}) copy-start(f32[192,1,128]{2,0,1:T(8,128)} %get-tuple-element.225) | copy-start | bytes 294916
  258.8 8.1 %copy-start.114 = (f32[192,1,128]{2,0,1:T(8,128)S(1)}, f32[192,1,128]{2,0,1:T(8,128)}, u32[]{:S(2)}) copy-start(f32[192,1,128]{2,0,1:T(8,128)} %get-tuple-element.226) | copy-start | bytes 294916
  258.8 8.1 %copy-start.115 = (f32[192,1,128]{2,0,1:T(8,128)S(1)}, f32[192,1,128]{2,0,1:T(8,128)}, u32[]{:S(2)}) copy-start(f32[192,1,128]{2,0,1:T(8,128)} %get-tuple-element.227) | copy-start | bytes 294916
  258.9 8.1 %copy-start.116 = (f32[192,1,128]{2,0,1:T(8,128)S(1)}, f32[192,1,128]{2,0,1:T(8,128)}, u32[]{:S(2)}) copy-start(f32[192,1,128]{2,0,1:T(8,128)} %get-tuple-element.228) | copy-start | bytes 294916
  258.9 8.1 %copy-start.117 = (f32[192,1,128]{2,0,1:T(8,128)S(1)}, f32[192,1,128]{2,0,1:T(8,128)}, u32[]{:S(2)}) copy-start(f32[192,1,128]{2,0,1:T(8,128)} %get-tuple-element.229) | copy-start | bytes 294916
  258.9 8.1 %copy-start.118 = (f32[192,1,128]{2,0,1:T(8,128)S(1)}, f32[192,1,128]{2,0,1:T(8,128)}, u32[]{:S(2)}) copy-start(f32[192,1,128]{2,0,1:T(8,128)} %get-tuple-element.230) | copy-start | bytes 294916
  258.9 8.1 %copy-start.119 = (f32[192,1,128]{2,0,1:T(8,128)S(1)}, f32[192,1,128]{2,0,1:T(8,128)}, u32[]{:S(2)}) copy-start(f32[192,1,128]{2,0,1:T(8,128)} %get-tuple-element.231) | copy-start | bytes 294916
  258.9 8.1 %copy-start.120 = (f32[192,1,128]{2,0,1:T(8,128)S(1)}, f32[192,1,128]{2,0,1:T(8,128)}, u32[]{:S(2)}) copy-start(f32[192,1,128]{2,0,1:T(8,128)} %get-tuple-element.232) | copy-start | bytes 294916
  258.9 8.1 %copy-start.121 = (f32[192,1,128]{2,0,1:T(8,128)S(1)}, f32[192,1,128]{2,0,1:T(8,128)}, u32[]{:S(2)}) copy-start(f32[192,1,128]{2,0,1:T(8,128)} %get-tuple-element.233) | copy-start | bytes 294916
  258.9 8.1 %copy-start.122 = (f32[192,1,128]{2,0,1:T(8,128)S(1)}, f32[192,1,128]{2,0,1:T(8,128)}, u32[]{:S(2)}) copy-start(f32[192,1,128]{2,0,1:T(8,128)} %get-tuple-element.216) | copy-start | bytes 294916
  258.9 8.1 %copy-start.123 = (f32[192,1,128]{2,0,1:T(8,128)S(1)}, f32[192,1,128]{2,0,1:T(8,128)}, u32[]{:S(2)}) copy-start(f32[192,1,128]{2,0,1:T(8,128)} %get-tuple-element.217) | copy-start | bytes 294916
  258.9 8.1 %copy-start.124 = (f32[192,1,128]{2,0,1:T(8,128)S(1)}, f32[192,1,128]{2,0,1:T(8,128)}, u32[]{:S(2)}) copy-start(f32[192,1,128]{2,0,1:T(8,128)} %get-tuple-element.218) | copy-start | bytes 294916
  309.8 5.1 %collective-permute-start.2 = (bf16[8,3200]{1,0:T(8,128)(2,1)S(1)}, bf16[8,3200]{1,0:T(8,128)(2,1)S(1)}, u32[]{:S(2)}, u32[]{:S(2)}) collective-permute-start(bf16[8,3200]{1,0:T(8,128)(2,1)S(1)} %get-tuple-element.340), channel_id=1, source_target_pairs={{0,1},{1,2},{2,3},{3,4},{4,5},{5,6},{6,7},{7,0},{8,9},{9,10},{10,1... | collective-permute-start | bytes 153608 | tf_op jit(solution)/shard_map/ppermute | solution.py:14
  309.9 5.0 %collective-permute-start.3 = (bf16[8,3200]{1,0:T(8,128)(2,1)S(1)}, bf16[8,3200]{1,0:T(8,128)(2,1)S(1)}, u32[]{:S(2)}, u32[]{:S(2)}) collective-permute-start(bf16[8,3200]{1,0:T(8,128)(2,1)S(1)} %get-tuple-element.341), channel_id=1, source_target_pairs={{1,0},{2,1},{3,2},{4,3},{5,4},{6,5},{7,6},{0,7},{9,8},{10,9},{11,1... | collective-permute-start | bytes 153608 | tf_op jit(solution)/shard_map/ppermute | solution.py:17
  314.9 152.6 %copy-start.1 = (f32[1,16,1600]{2,1,0:T(8,128)S(1)}, f32[1,16,1600]{2,1,0:T(8,128)}, u32[]{:S(2)}) copy-start(f32[1,16,1600]{2,1,0:T(8,128)} %param.17) | copy-start | bytes 307204
  (488 other events, 1625.3 us)
Sparse Core Ops, SparseCore 0:
  9.9 26.5 all-gather.1
  312.7 145.4 all-reduce.275
where the time goes:
time: 482 us; the launch traced here: 475 us
  waiting for transfers between devices  141 us (29%)
  other arithmetic  119 us (25%)
  blocking collectives  95.7 us (20%)
  local copies, waits for them, and re-layouts  58.4 us (12%)
  matrix products  31.6 us (7%)
  between operations  22.2 us (5%)
  starting transfers between devices  6.1 us (1%)
    psum x1, waiting for transfers between devices, body(): grand_totals = lax.psum(grad_terms, ('dp', 'graph'))  141 us
    psum x1, blocking collectives, body(): grand_totals = lax.psum(grad_terms, ('dp', 'graph'))  40.3 us
    scatter-add x4, other arithmetic, attend(): jnp.take(coeffs[:, degree * degree:(degree + 1) * (degree + 1), :], edge_...  35.1 us
    mul x13, other arithmetic, apply_block(): total = total + block[row, column][:, None] * source_part[:, column, :]  17.5 us
    unnamed x26, other arithmetic  15.7 us
    all_gather x1, blocking collectives, body(): lax.all_gather(w_one_re, 'graph', axis=0, tiled=True)  10.2 us
    all_gather x1, blocking collectives, body(): lax.all_gather(w_two_re, 'graph', axis=0, tiled=True)  10.1 us
    dynamic_slice x7, local copies, waits for them, and re-layouts, body(): lax.dynamic_slice_in_dim(summed_all, position * shard_ref.shape[0], shard...  9.83 us
  transfers between devices with their start and end apart: 6, of which 1 were waited for; matrix products, arithmetic and copies ran while one was open for 12% of the time, Pallas kernels for 0%

commit v1 on v0

--- a/solution.py
+++ b/solution.py
@@ -225,7 +225,7 @@
     grad_features = collected[:atom_count][None]
     grad_terms = tuple((term.astype(jnp.float32) for term in pulled[1:]))
     shard_refs = (w_zero, w_one_re, w_one_im, w_two_re, w_two_im, w_target, alpha_vec)
-    grand_totals = lax.psum(grad_terms, ("dp", "graph"))
+    grand_totals = jax.lax.psum(jax.lax.psum(grad_terms, axis_name="graph"), axis_name="dp")
     position = lax.axis_index("graph")
     shards = tuple(
         (

time: 482 us -> 535 us (1.11)
  waiting for transfers between devices: 141 us -> 195 us
    psum x1 -> x2, waiting for transfers between devices: 141 us -> 195 us  [the longest x1 112 us: body(): jax.lax.psum(jax.lax.psum(grad_terms, axis_name='graph'), axis_name='dp')]
    psum x1 -> x2, blocking collectives: 40.3 us -> 44 us  [the longest x1 23.5 us: body(): jax.lax.psum(grad_terms, axis_name='graph')]
    unnamed x1103 -> x1171, local copies, waits for them, and re-layouts: 9.68 us -> 11.4 us
  transfers between devices with their start and end apart: 6 -> 7, of which waited for: 1 -> 2; matrix products, arithmetic and copies ran while one was open for 12% -> 12% of each run, Pallas kernels for 0% -> 0%
where the time goes in v1:
time: 535 us; the launch traced here: 529 us
  waiting for transfers between devices  195 us (36%)
  other arithmetic  119 us (22%)
  blocking collectives  99.5 us (19%)
  local copies, waits for them, and re-layouts  57.4 us (11%)
  matrix products  29 us (5%)
  between operations  22.6 us (4%)
  starting transfers between devices  6.17 us (1%)
    psum x1, waiting for transfers between devices, body(): jax.lax.psum(jax.lax.psum(grad_terms, axis_name='graph'), axis_name='dp')  112 us
    psum x1, waiting for transfers between devices, body(): jax.lax.psum(grad_terms, axis_name='graph')  82.6 us
    scatter-add x4, other arithmetic, attend(): jnp.take(coeffs[:, degree * degree:(degree + 1) * (degree + 1), :], edge_...  36.1 us
    psum x1, blocking collectives, body(): jax.lax.psum(grad_terms, axis_name='graph')  23.5 us
    psum x1, blocking collectives, body(): jax.lax.psum(jax.lax.psum(grad_terms, axis_name='graph'), axis_name='dp')  20.5 us
    mul x13, other arithmetic, apply_block(): total = total + block[row, column][:, None] * source_part[:, column, :]  17.4 us
    unnamed x1171, local copies, waits for them, and re-layouts  11.4 us
    unnamed x26, other arithmetic  11 us
  transfers between devices with their start and end apart: 7, of which 2 were waited for; matrix products, arithmetic and copies ran while one was open for 12% of the time, Pallas kernels for 0%

profile of v1, /device:TPU:0, one launch (start us, length us, event | category | flops | bytes accessed | tf_op | source)
XLA Modules:
  0.0 528.8 jit_solution(6878452874503521862)
XLA Ops:
  11.7 3.4 collective-permute-start.1
  25.2 9.0 %all_gather.23 = bf16[64,8]{1,0:T(8,128)(2,1)S(1)} all-gather(bf16[8,8]{1,0:T(8,128)(2,1)S(1)} %copy-done.573), channel_id=1, replica_groups=mesh['dp'=4,'graph'=8] {'graph'}, dimensions={0}, use_global_device_ids=true | all-gather | bytes 1152 | tf_op jit(solution)/shard_map/all_gather | solution.py:183
  35.5 8.3 %all_gather.22 = bf16[128,512]{1,0:T(8,128)(2,1)S(1)} all-gather(bf16[16,512]{1,0:T(8,128)(2,1)S(1)} %copy-done.560), channel_id=1, replica_groups=mesh['dp'=4,'graph'=8] {'graph'}, dimensions={0}, use_global_device_ids=true | all-gather | bytes 147456 | tf_op jit(solution)/shard_map/all_gather | solution.py:182
  43.9 10.1 %all_gather.26 = bf16[384,192]{1,0:T(8,128)(2,1)} all-gather(bf16[48,192]{1,0:T(8,128)(2,1)S(1)} %copy-done.556), channel_id=1, replica_groups=mesh['dp'=4,'graph'=8] {'graph'}, dimensions={0}, use_global_device_ids=true | all-gather | bytes 165888 | tf_op jit(solution)/shard_map/all_gather | solution.py:180
  54.0 8.3 %all_gather.27 = bf16[384,192]{1,0:T(8,128)(2,1)S(1)} all-gather(bf16[48,192]{1,0:T(8,128)(2,1)S(1)} %copy-done.557), channel_id=1, replica_groups=mesh['dp'=4,'graph'=8] {'graph'}, dimensions={0}, use_global_device_ids=true | all-gather | bytes 165888 | tf_op jit(solution)/shard_map/all_gather | solution.py:181
  62.4 10.2 %all_gather.24 = bf16[512,256]{1,0:T(8,128)(2,1)} all-gather(bf16[64,256]{1,0:T(8,128)(2,1)S(1)} %copy-done.200), channel_id=1, replica_groups=mesh['dp'=4,'graph'=8] {'graph'}, dimensions={0}, use_global_device_ids=true | all-gather | bytes 294912 | tf_op jit(solution)/shard_map/all_gather | solution.py:178
  72.5 9.6 %all_gather.25 = bf16[512,256]{1,0:T(8,128)(2,1)} all-gather(bf16[64,256]{1,0:T(8,128)(2,1)S(1)} %copy-done.201), channel_id=1, replica_groups=mesh['dp'=4,'graph'=8] {'graph'}, dimensions={0}, use_global_device_ids=true | all-gather | bytes 294912 | tf_op jit(solution)/shard_map/all_gather | solution.py:179
  86.5 1.8 gather_fusion.5
  94.0 1.3 pad_maximum_fusion.9
  96.9 1.5 pad_maximum_fusion.1
  105.3 2.0 gather_fusion.4
  107.5 1.7 copy_select_fusion
  113.5 1.5 multiply_add_fusion.14
  115.1 1.6 constant_dynamic-update-slice_fusion.2
  117.6 1.7 constant_dynamic-update-slice_fusion
  119.8 1.7 convolution_subtract_fusion.1
  123.2 1.1 copy.178
  129.6 1.8 fusion.145
  144.2 1.9 multiply_reduce_fusion.10
  146.2 1.1 multiply_reduce_fusion.2
  147.5 1.6 slice_multiply_fusion
  149.4 1.5 scatter_custom_fusion
  152.1 1.2 broadcast_add_fusion
  157.1 1.4 fusion.3
  158.5 1.3 copy.189
  160.6 1.6 copy.223
  162.3 2.1 fusion.11
  164.3 2.0 fusion.9
  166.3 1.2 reshape.3776
  167.5 1.1 reshape.3778
  171.8 1.2 slice_multiply_fusion.89
  173.2 1.3 slice_multiply_fusion.98
  174.6 1.2 slice_multiply_fusion.107
  175.9 1.9 slice_multiply_fusion.116
  177.9 1.9 slice_multiply_fusion.125
  181.7 1.8 slice_multiply_fusion.49
  183.7 1.2 slice_multiply_fusion.56
  185.0 1.3 slice_multiply_fusion.63
  186.4 1.2 slice_multiply_fusion.70
  190.7 1.8 slice_multiply_fusion.30
  192.6 1.2 slice_multiply_fusion.35
  193.9 1.9 fusion.2
  200.2 2.1 scatter_custom_fusion.6
  202.5 1.1 fusion.7
  204.6 2.2 scatter_custom_fusion.1
  206.8 1.6 fusion.17
  218.4 2.0 pad_add_fusion
  222.2 1.9 pad_add_fusion.4
  224.1 1.3 copy.197
  225.8 1.2 copy.203
  227.0 7.2 %scatter_fusion.3 = f32[32,3,128]{2,1,0:T(4,128)S(1)} fusion(f32[32,3,128]{2,1,0:T(4,128)S(1)} %broadcast_in_dim.136, s32[192]{0:T(256)S(1)} %bitcast.473, f32[192,3,128]{2,1,0:T(4,128)S(1)} %copy.207), kind=kCustom, calls=%fused_computation.14 | custom fusion | flops 73728 | bytes 885504 | tf_op jit(solution)/shard_map/transpose(jvp(jit(_take)))/scatter-add | solution.py:85
  234.2 7.6 %scatter_fusion = f32[32,9,128]{2,1,0:T(8,128)S(1)} fusion(f32[32,9,128]{2,1,0:T(8,128)S(1)} %broadcast_in_dim.133, s32[192]{0:T(256)S(1)} %bitcast.474, f32[192,9,128]{2,1,0:T(8,128)S(1)} %copy.191), kind=kCustom, calls=%fused_computation.11 | custom fusion | flops 221184 | bytes 2654976 | tf_op jit(solution)/shard_map/transpose(jvp(jit(_take)))/scatter-add | solution.py:85
  241.9 14.0 %scatter_fusion.1 = f32[32,7,128]{2,1,0:T(8,128)S(1)} fusion(f32[32,7,128]{2,1,0:T(8,128)S(1)} %broadcast_in_dim.134, s32[192]{0:T(256)S(1)} %bitcast.475, f32[192,7,128]{2,1,0:T(8,128)} %copy.197), kind=kCustom, calls=%fused_computation.12 | custom fusion | flops 172032 | bytes 2065152 | tf_op jit(solution)/shard_map/transpose(jvp(jit(_take)))/scatter-add | solution.py:85
  256.0 7.2 %scatter_fusion.2 = f32[32,5,128]{2,1,0:T(8,128)S(1)} fusion(f32[32,5,128]{2,1,0:T(8,128)S(1)} %broadcast_in_dim.135, s32[192]{0:T(256)S(1)} %bitcast.476, f32[192,5,128]{2,1,0:T(8,128)S(1)} %copy-done.4), kind=kCustom, calls=%fused_computation.13 | custom fusion | flops 122880 | bytes 1475328 | tf_op jit(solution)/shard_map/transpose(jvp(jit(_take)))/scatter-add | solution.py:85
  264.6 82.6 %all-reduce.278.cloned.1.call-done = (f32[640,832]{1,0:T(8,128)}, f32[512,256]{1,0:T(8,128)}, f32[512,256]{1,0:T(8,128)}, f32[384,192]{1,0:T(8,128)}, f32[384,192]{1,0:T(8,128)}, /*index=5*/f32[128,512]{0,1:T(8,128)}) async-done(((f32[640,832]{1,0:T(8,128)}, f32[512,256]{1,0:T(8,128)}, f32[512,256]{1,0:T(8,128)}, f32[384,192]{1,0:T(8,128)}, f32[384,192]{1,0:T(8,128)}, /*index=5*/f32[128,512]{0,1:T(8,128)}), ...) | async-done | bytes 4030480 | tf_op jit(solution)/shard_map/psum | solution.py:228
  348.3 2.6 collective-permute-start.3
  350.9 23.5 %psum.110 = f32[64,8]{1,0:T(8,128)S(1)} all-reduce(f32[64,8]{1,0:T(8,128)S(1)} %convert_bitcast_fusion), channel_id=1, replica_groups=mesh['dp'=4,'graph'=8] {'graph'}, use_global_device_ids=true, to_apply=%region_36.38 | all-reduce | flops 512 | bytes 4096 | tf_op jit(solution)/shard_map/psum | solution.py:228
  374.4 20.5 %psum.111 = f32[64,8]{1,0:T(8,128)S(1)} all-reduce(f32[64,8]{1,0:T(8,128)S(1)} %psum.110), channel_id=1, replica_groups=mesh['dp'=4,'graph'=8] {'dp'}, use_global_device_ids=true, to_apply=%region_37.39 | all-reduce | flops 512 | bytes 4096 | tf_op jit(solution)/shard_map/psum | solution.py:228
  400.7 112.1 %all-reduce.280.cloned.1.call-done = (f32[640,832]{1,0:T(8,128)}, f32[512,256]{1,0:T(8,128)}, f32[512,256]{1,0:T(8,128)}, f32[384,192]{1,0:T(8,128)}, f32[384,192]{1,0:T(8,128)}, /*index=5*/f32[128,512]{0,1:T(8,128)}) async-done(((f32[640,832]{1,0:T(8,128)}, f32[512,256]{1,0:T(8,128)}, f32[512,256]{1,0:T(8,128)}, f32[384,192]{1,0:T(8,128)}, f32[384,192]{1,0:T(8,128)}, /*index=5*/f32[128,512]{0,1:T(8,128)}), ...) | async-done | bytes 4030480 | tf_op jit(solution)/shard_map/psum | solution.py:228
  512.7 1.4 constant_dynamic-slice_fusion.3
  514.1 1.4 constant_dynamic-slice_fusion.2
  515.6 1.5 constant_dynamic-slice_fusion.5
  517.0 1.5 constant_dynamic-slice_fusion.4
  520.3 1.7 constant_dynamic-slice_fusion.6
  (1381 shorter events, 95.1 us)
Async XLA Ops:
  7.2 75.1 %copy-start = (f32[1,16,1600]{2,1,0:T(8,128)S(1)}, f32[1,16,1600]{2,1,0:T(8,128)}, u32[]{:S(2)}) copy-start(f32[1,16,1600]{2,1,0:T(8,128)} %param.17) | copy-start | bytes 307204
  7.2 122.4 %all-gather.2.cloned.1.call-start = ((), (), s32[]{:S(2)}) async-start(), calls=%async_computation | async-start | bytes 1290240 | tf_op jit(solution)/shard_map/all_gather | solution.py:177
  8.0 339.3 %all-reduce.278.cloned.1.call-start = ((), (), s32[]{:S(2)}) async-start(), calls=%async_computation.1 | async-start | bytes 8781824 | tf_op jit(solution)/shard_map/psum | solution.py:228
  11.7 81.6 %collective-permute-start.1 = (f32[8,3200]{1,0:T(8,128)}, f32[8,3200]{1,0:T(8,128)}, u32[]{:S(2)}, u32[]{:S(2)}) collective-permute-start(f32[8,3200]{1,0:T(8,128)} %broadcast_select_fusion), channel_id=1, source_target_pairs={{1,0},{2,1},{3,2},{4,3},{5,4},{6,5},{7,6},{0,7},{9,8},{10,9},{11,1... | collective-permute-start | bytes 307208 | tf_op jit(solution)/shard_map/ppermute | solution.py:17
  15.7 56.8 %copy-start.201 = (bf16[64,256]{1,0:T(8,128)(2,1)S(1)}, bf16[64,256]{1,0:T(8,128)(2,1)}, u32[]{:S(2)}) copy-start(bf16[64,256]{1,0:T(8,128)(2,1)} %param.25) | copy-start | bytes 98308
  16.4 76.9 %collective-permute-start = (f32[8,3200]{1,0:T(8,128)}, f32[8,3200]{1,0:T(8,128)}, u32[]{:S(2)}, u32[]{:S(2)}) collective-permute-start(f32[8,3200]{1,0:T(8,128)} %broadcast_select_fusion.1), channel_id=1, source_target_pairs={{0,1},{1,2},{2,3},{3,4},{4,5},{5,6},{6,7},{7,0},{8,9},{9,10},{10,1... | collective-permute-start | bytes 307208 | tf_op jit(solution)/shard_map/ppermute | solution.py:14
  18.4 98.3 %copy-start.204 = (f32[1,1,192]{2,1,0:T(1,128)}, f32[1,1,192]{2,1,0:T(1,128)S(1)}, u32[]{:S(2)}) copy-start(f32[1,1,192]{2,1,0:T(1,128)S(1)} %get-tuple-element.461) | copy-start | bytes 2308
  19.0 64.2 %copy-start.241 = (f32[1,1,192]{2,1,0:T(1,128)}, f32[1,1,192]{2,1,0:T(1,128)S(1)}, u32[]{:S(2)}) copy-start(f32[1,1,192]{2,1,0:T(1,128)S(1)} %get-tuple-element.430) | copy-start | bytes 2308
  19.0 64.5 %copy-start.229 = (f32[1,1,192]{2,1,0:T(1,128)}, f32[1,1,192]{2,1,0:T(1,128)S(1)}, u32[]{:S(2)}) copy-start(f32[1,1,192]{2,1,0:T(1,128)S(1)} %get-tuple-element.429) | copy-start | bytes 2308
  19.1 66.1 %copy-start.253 = (f32[1,1,192]{2,1,0:T(1,128)}, f32[1,1,192]{2,1,0:T(1,128)S(1)}, u32[]{:S(2)}) copy-start(f32[1,1,192]{2,1,0:T(1,128)S(1)} %get-tuple-element.431) | copy-start | bytes 2308
  19.1 66.1 %copy-start.258 = (f32[1,1,192]{2,1,0:T(1,128)}, f32[1,1,192]{2,1,0:T(1,128)S(1)}, u32[]{:S(2)}) copy-start(f32[1,1,192]{2,1,0:T(1,128)S(1)} %get-tuple-element.432) | copy-start | bytes 2308
  19.1 66.1 %copy-start.263 = (f32[1,1,192]{2,1,0:T(1,128)}, f32[1,1,192]{2,1,0:T(1,128)S(1)}, u32[]{:S(2)}) copy-start(f32[1,1,192]{2,1,0:T(1,128)S(1)} %get-tuple-element.433) | copy-start | bytes 2308
  19.1 66.1 %copy-start.219 = (f32[1,1,192]{2,1,0:T(1,128)}, f32[1,1,192]{2,1,0:T(1,128)S(1)}, u32[]{:S(2)}) copy-start(f32[1,1,192]{2,1,0:T(1,128)S(1)} %get-tuple-element.428) | copy-start | bytes 2308
  20.5 62.7 %copy-start.293 = (f32[1,1,192]{2,1,0:T(1,128)}, f32[1,1,192]{2,1,0:T(1,128)S(1)}, u32[]{:S(2)}) copy-start(f32[1,1,192]{2,1,0:T(1,128)S(1)} %get-tuple-element.411) | copy-start | bytes 2308
  20.5 62.7 %copy-start.305 = (f32[1,1,192]{2,1,0:T(1,128)}, f32[1,1,192]{2,1,0:T(1,128)S(1)}, u32[]{:S(2)}) copy-start(f32[1,1,192]{2,1,0:T(1,128)S(1)} %get-tuple-element.412) | copy-start | bytes 2308
  20.6 62.7 %copy-start.321 = (f32[1,1,192]{2,1,0:T(1,128)}, f32[1,1,192]{2,1,0:T(1,128)S(1)}, u32[]{:S(2)}) copy-start(f32[1,1,192]{2,1,0:T(1,128)S(1)} %get-tuple-element.413) | copy-start | bytes 2308
  23.3 59.4 %copy-start.572 = (s32[192,1]{0,1:T(1,128)}, s32[192,1]{0,1:T(1,128)S(1)}, u32[]{:S(2)}) copy-start(s32[192,1]{0,1:T(1,128)S(1)} %get-tuple-element.477) | copy-start | bytes 2308
  23.3 70.0 %copy-start.198 = (s32[192,1]{0,1:T(1,128)}, s32[192,1]{0,1:T(1,128)S(1)}, u32[]{:S(2)}) copy-start(s32[192,1]{0,1:T(1,128)S(1)} %get-tuple-element.478) | copy-start | bytes 2308
  25.2 58.1 %copy-start.527 = (f32[1,1,192]{2,1,0:T(1,128)}, f32[1,1,192]{2,1,0:T(1,128)S(1)}, u32[]{:S(2)}) copy-start(f32[1,1,192]{2,1,0:T(1,128)S(1)} %get-tuple-element.469) | copy-start | bytes 2308
  25.2 58.2 %copy-start.535 = (f32[1,1,192]{2,1,0:T(1,128)}, f32[1,1,192]{2,1,0:T(1,128)S(1)}, u32[]{:S(2)}) copy-start(f32[1,1,192]{2,1,0:T(1,128)S(1)} %get-tuple-element.470) | copy-start | bytes 2308
  25.2 58.2 %copy-start.545 = (f32[1,1,192]{2,1,0:T(1,128)}, f32[1,1,192]{2,1,0:T(1,128)S(1)}, u32[]{:S(2)}) copy-start(f32[1,1,192]{2,1,0:T(1,128)S(1)} %get-tuple-element.468) | copy-start | bytes 2308
  25.2 58.2 %copy-start.549 = (f32[1,1,192]{2,1,0:T(1,128)}, f32[1,1,192]{2,1,0:T(1,128)S(1)}, u32[]{:S(2)}) copy-start(f32[1,1,192]{2,1,0:T(1,128)S(1)} %get-tuple-element.471) | copy-start | bytes 2308
  25.2 58.2 %copy-start.553 = (f32[1,1,192]{2,1,0:T(1,128)}, f32[1,1,192]{2,1,0:T(1,128)S(1)}, u32[]{:S(2)}) copy-start(f32[1,1,192]{2,1,0:T(1,128)S(1)} %get-tuple-element.476) | copy-start | bytes 2308
  263.3 249.4 %all-reduce.280.cloned.1.call-start = ((), (), s32[]{:S(2)}) async-start(), calls=%async_computation.2 | async-start | bytes 8781824 | tf_op jit(solution)/shard_map/psum | solution.py:228
  347.3 47.7 %copy-start.454 = (f32[1,1,192]{2,1,0:T(1,128)S(1)}, f32[1,1,192]{2,1,0:T(1,128)}, u32[]{:S(2)}) copy-start(f32[1,1,192]{2,1,0:T(1,128)} %get-tuple-element.374) | copy-start | bytes 2308
  347.3 48.4 %copy-start.347 = (f32[1,1,192]{2,1,0:T(1,128)S(1)}, f32[1,1,192]{2,1,0:T(1,128)}, u32[]{:S(2)}) copy-start(f32[1,1,192]{2,1,0:T(1,128)} %get-tuple-element.400) | copy-start | bytes 2308
  347.3 48.4 %copy-start.434 = (f32[1,1,192]{2,1,0:T(1,128)S(1)}, f32[1,1,192]{2,1,0:T(1,128)}, u32[]{:S(2)}) copy-start(f32[1,1,192]{2,1,0:T(1,128)} %get-tuple-element.364) | copy-start | bytes 2308
  347.3 48.4 %copy-start.438 = (f32[1,1,192]{2,1,0:T(1,128)S(1)}, f32[1,1,192]{2,1,0:T(1,128)}, u32[]{:S(2)}) copy-start(f32[1,1,192]{2,1,0:T(1,128)} %get-tuple-element.373) | copy-start | bytes 2308
  347.3 48.4 %copy-start.472 = (f32[1,1,192]{2,1,0:T(1,128)S(1)}, f32[1,1,192]{2,1,0:T(1,128)}, u32[]{:S(2)}) copy-start(f32[1,1,192]{2,1,0:T(1,128)} %get-tuple-element.382) | copy-start | bytes 2308
  347.3 48.4 %copy-start.475 = (f32[1,1,192]{2,1,0:T(1,128)S(1)}, f32[1,1,192]{2,1,0:T(1,128)}, u32[]{:S(2)}) copy-start(f32[1,1,192]{2,1,0:T(1,128)} %get-tuple-element.391) | copy-start | bytes 2308
  347.3 48.4 %copy-start.344 = (f32[1,1,192]{2,1,0:T(1,128)S(1)}, f32[1,1,192]{2,1,0:T(1,128)}, u32[]{:S(2)}) copy-start(f32[1,1,192]{2,1,0:T(1,128)} %get-tuple-element.399) | copy-start | bytes 2308
  347.3 48.4 %copy-start.418 = (f32[1,1,192]{2,1,0:T(1,128)S(1)}, f32[1,1,192]{2,1,0:T(1,128)}, u32[]{:S(2)}) copy-start(f32[1,1,192]{2,1,0:T(1,128)} %get-tuple-element.363) | copy-start | bytes 2308
  347.4 48.4 %copy-start.422 = (f32[1,1,192]{2,1,0:T(1,128)S(1)}, f32[1,1,192]{2,1,0:T(1,128)}, u32[]{:S(2)}) copy-start(f32[1,1,192]{2,1,0:T(1,128)} %get-tuple-element.372) | copy-start | bytes 2308
  347.4 48.4 %copy-start.466 = (f32[1,1,192]{2,1,0:T(1,128)S(1)}, f32[1,1,192]{2,1,0:T(1,128)}, u32[]{:S(2)}) copy-start(f32[1,1,192]{2,1,0:T(1,128)} %get-tuple-element.381) | copy-start | bytes 2308
  347.4 48.4 %copy-start.470 = (f32[1,1,192]{2,1,0:T(1,128)S(1)}, f32[1,1,192]{2,1,0:T(1,128)}, u32[]{:S(2)}) copy-start(f32[1,1,192]{2,1,0:T(1,128)} %get-tuple-element.390) | copy-start | bytes 2308
  347.4 48.5 %copy-start.340 = (f32[1,1,192]{2,1,0:T(1,128)S(1)}, f32[1,1,192]{2,1,0:T(1,128)}, u32[]{:S(2)}) copy-start(f32[1,1,192]{2,1,0:T(1,128)} %get-tuple-element.398) | copy-start | bytes 2308
  347.4 48.5 %copy-start.399 = (f32[1,1,192]{2,1,0:T(1,128)S(1)}, f32[1,1,192]{2,1,0:T(1,128)}, u32[]{:S(2)}) copy-start(f32[1,1,192]{2,1,0:T(1,128)} %get-tuple-element.362) | copy-start | bytes 2308
  347.4 48.5 %copy-start.403 = (f32[1,1,192]{2,1,0:T(1,128)S(1)}, f32[1,1,192]{2,1,0:T(1,128)}, u32[]{:S(2)}) copy-start(f32[1,1,192]{2,1,0:T(1,128)} %get-tuple-element.371) | copy-start | bytes 2308
  347.4 48.5 %copy-start.458 = (f32[1,1,192]{2,1,0:T(1,128)S(1)}, f32[1,1,192]{2,1,0:T(1,128)}, u32[]{:S(2)}) copy-start(f32[1,1,192]{2,1,0:T(1,128)} %get-tuple-element.380) | copy-start | bytes 2308
  347.4 48.5 %copy-start.462 = (f32[1,1,192]{2,1,0:T(1,128)S(1)}, f32[1,1,192]{2,1,0:T(1,128)}, u32[]{:S(2)}) copy-start(f32[1,1,192]{2,1,0:T(1,128)} %get-tuple-element.389) | copy-start | bytes 2308
  348.0 48.0 %copy-start.336 = (f32[1,1,192]{2,1,0:T(1,128)S(1)}, f32[1,1,192]{2,1,0:T(1,128)}, u32[]{:S(2)}) copy-start(f32[1,1,192]{2,1,0:T(1,128)} %get-tuple-element.397) | copy-start | bytes 2308
  348.0 48.0 %copy-start.384 = (f32[1,1,192]{2,1,0:T(1,128)S(1)}, f32[1,1,192]{2,1,0:T(1,128)}, u32[]{:S(2)}) copy-start(f32[1,1,192]{2,1,0:T(1,128)} %get-tuple-element.361) | copy-start | bytes 2308
  348.0 48.0 %copy-start.388 = (f32[1,1,192]{2,1,0:T(1,128)S(1)}, f32[1,1,192]{2,1,0:T(1,128)}, u32[]{:S(2)}) copy-start(f32[1,1,192]{2,1,0:T(1,128)} %get-tuple-element.370) | copy-start | bytes 2308
  348.0 48.0 %copy-start.442 = (f32[1,1,192]{2,1,0:T(1,128)S(1)}, f32[1,1,192]{2,1,0:T(1,128)}, u32[]{:S(2)}) copy-start(f32[1,1,192]{2,1,0:T(1,128)} %get-tuple-element.379) | copy-start | bytes 2308
  348.0 48.0 %copy-start.446 = (f32[1,1,192]{2,1,0:T(1,128)S(1)}, f32[1,1,192]{2,1,0:T(1,128)}, u32[]{:S(2)}) copy-start(f32[1,1,192]{2,1,0:T(1,128)} %get-tuple-element.388) | copy-start | bytes 2308
  348.0 48.0 %copy-start.332 = (f32[1,1,192]{2,1,0:T(1,128)S(1)}, f32[1,1,192]{2,1,0:T(1,128)}, u32[]{:S(2)}) copy-start(f32[1,1,192]{2,1,0:T(1,128)} %get-tuple-element.396) | copy-start | bytes 2308
  348.0 48.0 %copy-start.376 = (f32[1,1,192]{2,1,0:T(1,128)S(1)}, f32[1,1,192]{2,1,0:T(1,128)}, u32[]{:S(2)}) copy-start(f32[1,1,192]{2,1,0:T(1,128)} %get-tuple-element.360) | copy-start | bytes 2308
  348.0 48.0 %copy-start.380 = (f32[1,1,192]{2,1,0:T(1,128)S(1)}, f32[1,1,192]{2,1,0:T(1,128)}, u32[]{:S(2)}) copy-start(f32[1,1,192]{2,1,0:T(1,128)} %get-tuple-element.369) | copy-start | bytes 2308
  348.0 48.0 %copy-start.426 = (f32[1,1,192]{2,1,0:T(1,128)S(1)}, f32[1,1,192]{2,1,0:T(1,128)}, u32[]{:S(2)}) copy-start(f32[1,1,192]{2,1,0:T(1,128)} %get-tuple-element.378) | copy-start | bytes 2308
  348.1 48.0 %copy-start.430 = (f32[1,1,192]{2,1,0:T(1,128)S(1)}, f32[1,1,192]{2,1,0:T(1,128)}, u32[]{:S(2)}) copy-start(f32[1,1,192]{2,1,0:T(1,128)} %get-tuple-element.387) | copy-start | bytes 2308
  348.1 48.1 %copy-start.368 = (f32[1,1,192]{2,1,0:T(1,128)S(1)}, f32[1,1,192]{2,1,0:T(1,128)}, u32[]{:S(2)}) copy-start(f32[1,1,192]{2,1,0:T(1,128)} %get-tuple-element.359) | copy-start | bytes 2308
  348.1 48.1 %copy-start.372 = (f32[1,1,192]{2,1,0:T(1,128)S(1)}, f32[1,1,192]{2,1,0:T(1,128)}, u32[]{:S(2)}) copy-start(f32[1,1,192]{2,1,0:T(1,128)} %get-tuple-element.368) | copy-start | bytes 2308
  348.1 48.1 %copy-start.407 = (f32[1,1,192]{2,1,0:T(1,128)S(1)}, f32[1,1,192]{2,1,0:T(1,128)}, u32[]{:S(2)}) copy-start(f32[1,1,192]{2,1,0:T(1,128)} %get-tuple-element.377) | copy-start | bytes 2308
  348.1 48.1 %copy-start.411 = (f32[1,1,192]{2,1,0:T(1,128)S(1)}, f32[1,1,192]{2,1,0:T(1,128)}, u32[]{:S(2)}) copy-start(f32[1,1,192]{2,1,0:T(1,128)} %get-tuple-element.386) | copy-start | bytes 2308
  348.1 48.1 %copy-start.414 = (f32[1,1,192]{2,1,0:T(1,128)S(1)}, f32[1,1,192]{2,1,0:T(1,128)}, u32[]{:S(2)}) copy-start(f32[1,1,192]{2,1,0:T(1,128)} %get-tuple-element.394) | copy-start | bytes 2308
  348.1 48.1 %copy-start.356 = (f32[1,1,192]{2,1,0:T(1,128)S(1)}, f32[1,1,192]{2,1,0:T(1,128)}, u32[]{:S(2)}) copy-start(f32[1,1,192]{2,1,0:T(1,128)} %get-tuple-element.358) | copy-start | bytes 2308
  348.1 48.1 %copy-start.360 = (f32[1,1,192]{2,1,0:T(1,128)S(1)}, f32[1,1,192]{2,1,0:T(1,128)}, u32[]{:S(2)}) copy-start(f32[1,1,192]{2,1,0:T(1,128)} %get-tuple-element.367) | copy-start | bytes 2308
  348.1 48.1 %copy-start.364 = (f32[1,1,192]{2,1,0:T(1,128)S(1)}, f32[1,1,192]{2,1,0:T(1,128)}, u32[]{:S(2)}) copy-start(f32[1,1,192]{2,1,0:T(1,128)} %get-tuple-element.375) | copy-start | bytes 2308
  348.1 48.1 %copy-start.392 = (f32[1,1,192]{2,1,0:T(1,128)S(1)}, f32[1,1,192]{2,1,0:T(1,128)}, u32[]{:S(2)}) copy-start(f32[1,1,192]{2,1,0:T(1,128)} %get-tuple-element.385) | copy-start | bytes 2308
  348.2 48.1 %copy-start.395 = (f32[1,1,192]{2,1,0:T(1,128)S(1)}, f32[1,1,192]{2,1,0:T(1,128)}, u32[]{:S(2)}) copy-start(f32[1,1,192]{2,1,0:T(1,128)} %get-tuple-element.393) | copy-start | bytes 2308
  348.2 48.1 %copy-start.566 = (s32[1,192]{1,0:T(1,128)S(1)}, s32[1,192]{1,0:T(1,128)}, u32[]{:S(2)}) copy-start(s32[1,192]{1,0:T(1,128)} %param.22) | copy-start | bytes 2308
  348.2 49.8 %collective-permute-start.2 = (bf16[8,3200]{1,0:T(8,128)(2,1)S(1)}, bf16[8,3200]{1,0:T(8,128)(2,1)S(1)}, u32[]{:S(2)}, u32[]{:S(2)}) collective-permute-start(bf16[8,3200]{1,0:T(8,128)(2,1)S(1)} %get-tuple-element.346), channel_id=1, source_target_pairs={{0,1},{1,2},{2,3},{3,4},{4,5},{5,6},{6,7},{7,0},{8,9},{9,10},{10,1... | collective-permute-start | bytes 153608 | tf_op jit(solution)/shard_map/ppermute | solution.py:14
  348.3 49.8 %collective-permute-start.3 = (bf16[8,3200]{1,0:T(8,128)(2,1)S(1)}, bf16[8,3200]{1,0:T(8,128)(2,1)S(1)}, u32[]{:S(2)}, u32[]{:S(2)}) collective-permute-start(bf16[8,3200]{1,0:T(8,128)(2,1)S(1)} %get-tuple-element.347), channel_id=1, source_target_pairs={{1,0},{2,1},{3,2},{4,3},{5,4},{6,5},{7,6},{0,7},{9,8},{10,9},{11,1... | collective-permute-start | bytes 153608 | tf_op jit(solution)/shard_map/ppermute | solution.py:17
  398.0 124.0 %copy-start.1 = (f32[1,16,1600]{2,1,0:T(8,128)S(1)}, f32[1,16,1600]{2,1,0:T(8,128)}, u32[]{:S(2)}) copy-start(f32[1,16,1600]{2,1,0:T(8,128)} %param.17) | copy-start | bytes 307204
  (523 other events, 2176.5 us)
Sparse Core Ops, SparseCore 0:
  9.9 26.5 all-gather.1
  263.5 83.7 all-reduce.277
  350.1 162.5 all-reduce.279
